TPU v7x, 256 devices: a whole 4x4x8 slice. The times are simulated.
256 devices in a mesh: seq: 32 (over x_lo, z, core), tp: 8 (over y, x_hi).
Axes of the slice: x: 4 (x_hi: 2, x_lo: 2; x = x_hi * 2 + x_lo), y: 4, z: 8, core: 2. Of those that a mesh axis runs over, the one named last changes fastest.
Arguments:
- values: bfloat16 [8192, 4096], P('seq', 'tp'), may hold values from -6 to 6
- gate: bfloat16 [8192, 4096], P('seq', 'tp'), may hold values from -6 to 6
- out_grad: bfloat16 [8192, 4096], P('seq', 'tp'), may hold values from -6 to 6
- out_weight: bfloat16 [4096, 4096], P(None, 'tp'), may hold values from -0.09375 to 0.09375
- filt: float32 [8192, 4096], P('seq', 'tp'), may hold values from -6 to 6
- decay: float32 [4096], P('tp'), may hold values from 0.5 to 16
Outputs:
- d_values: bfloat16 [8192, 4096], P('seq', 'tp')
- d_gate: bfloat16 [8192, 4096], P('seq', 'tp')
- d_filt: float32 [8192, 4096], P('seq', 'tp')
- decay_grad: float32 [4096], P('tp')
- d_out_weight: float32 [4096, 4096], P('seq', 'tp')
All inputs are finite; a program needn't handle non-finite values.
Results may differ from a plain program's by a relative error of at most 0.0085.
Values may be sent and summed in bfloat16 or wider, within the bound.
A program may use at most 128 MiB of HBM per device.

v0:
```python
import math
import jax
import jax.numpy as jnp
from jax import lax
from jax.sharding import PartitionSpec as P

HIGHEST = lax.Precision.HIGHEST
TWO_PI = 2.0 * math.pi


def angles(left_idx, right_idx, modulus):
    index = left_idx[:, None] * right_idx[None, :] % modulus
    phase = index.astype(jnp.float32) * (TWO_PI / modulus)
    return (jnp.cos(phase), jnp.sin(phase))


def forward_outer(block, outer_cos, outer_sin, twid_cos, twid_sin):
    real_part = jnp.einsum("kp,fprc->fkrc", outer_cos, block, precision=HIGHEST)
    imag_part = -jnp.einsum("kp,fprc->fkrc", outer_sin, block, precision=HIGHEST)
    cos_b = twid_cos[None, :, :, None]
    sin_b = twid_sin[None, :, :, None]
    return jnp.stack([real_part * cos_b + imag_part * sin_b, imag_part * cos_b - real_part * sin_b])


def forward_inner(block, inner_cos, inner_sin):
    shape = block.shape
    merged = block.reshape(shape[0], shape[1], shape[2], shape[3] * shape[4], shape[5])
    real_in = merged[0]
    imag_in = merged[1]
    real_out = jnp.einsum("kb,fjbc->fjkc", inner_cos, real_in, precision=HIGHEST) + jnp.einsum(
        "kb,fjbc->fjkc", inner_sin, imag_in, precision=HIGHEST
    )
    imag_out = jnp.einsum("kb,fjbc->fjkc", inner_cos, imag_in, precision=HIGHEST) - jnp.einsum(
        "kb,fjbc->fjkc", inner_sin, real_in, precision=HIGHEST
    )
    return jnp.stack([real_out, imag_out])


def products(spectrum):
    real_v, real_k, real_g = (spectrum[0, 0], spectrum[0, 1], spectrum[0, 2])
    imag_v, imag_k, imag_g = (spectrum[1, 0], spectrum[1, 1], spectrum[1, 2])
    real_out = jnp.stack(
        [
            real_v * real_k - imag_v * imag_k,
            real_k * real_g + imag_k * imag_g,
            real_v * real_g + imag_v * imag_g,
        ]
    )
    imag_out = jnp.stack(
        [
            real_v * imag_k + imag_v * real_k,
            real_k * imag_g - imag_k * real_g,
            real_v * imag_g - imag_v * real_g,
        ]
    )
    return jnp.stack([real_out, imag_out])


def inverse_inner(spectrum, inner_cos, inner_sin, twid_cos, twid_sin):
    real_in = spectrum[0]
    imag_in = spectrum[1]
    real_mid = jnp.einsum("bk,fjkc->fjbc", inner_cos, real_in, precision=HIGHEST) - jnp.einsum(
        "bk,fjkc->fjbc", inner_sin, imag_in, precision=HIGHEST
    )
    imag_mid = jnp.einsum("bk,fjkc->fjbc", inner_cos, imag_in, precision=HIGHEST) + jnp.einsum(
        "bk,fjkc->fjbc", inner_sin, real_in, precision=HIGHEST
    )
    cos_b = twid_cos[None, :, :, None]
    sin_b = twid_sin[None, :, :, None]
    return jnp.stack([real_mid * cos_b - imag_mid * sin_b, real_mid * sin_b + imag_mid * cos_b])


def inverse_outer(block, back_cos, back_sin, padded):
    shape = block.shape
    merged = block.reshape(shape[0], shape[1], shape[2] * shape[3], shape[4], shape[5])
    result = jnp.einsum("pk,fkrc->fprc", back_cos, merged[0], precision=HIGHEST) - jnp.einsum(
        "pk,fkrc->fprc", back_sin, merged[1], precision=HIGHEST
    )
    return result / padded


def home_inputs(gate, grad_y, filt, decay, my_index, tok_rows, length, norm_scale):
    position = (
        (my_index * tok_rows + jnp.arange(tok_rows, dtype=jnp.int32)).astype(jnp.float32) / length
    )[:, None]
    window = jnp.exp(-decay[None, :] * position)
    kernel = filt * window * norm_scale
    gated_grad = grad_y.astype(jnp.float32) * gate.astype(jnp.float32)
    return (position, window, kernel, gated_grad)


def home_results(
    conv_out, conv_grad, kernel_grad, gate, grad_y, position, window, kernel, norm_scale
):
    d_values = conv_grad.astype(jnp.bfloat16)
    d_gate = (grad_y.astype(jnp.float32) * conv_out).astype(jnp.bfloat16)
    gated_out = (gate.astype(jnp.float32) * conv_out).astype(jnp.bfloat16)
    d_filt = kernel_grad * window * norm_scale
    decay_part = jnp.sum(position * kernel_grad * kernel, axis=0)
    return (d_values, d_gate, gated_out, d_filt, decay_part)


def on_device(values, gate, out_grad, out_weight, filt, decay):
    tok_rows = values.shape[0]
    seq_parts = lax.axis_size("seq")
    my_index = lax.axis_index("seq")
    sub_rows = tok_rows // seq_parts
    length = tok_rows * seq_parts
    padded = 2 * length
    norm_scale = 1.0 / math.sqrt(length)
    full_grad = lax.all_gather(out_grad, "tp", axis=1, tiled=True)
    grad_y = jnp.dot(full_grad, out_weight, preferred_element_type=jnp.float32).astype(jnp.bfloat16)
    outer_cos, outer_sin = angles(
        jnp.arange(2 * seq_parts, dtype=jnp.int32),
        jnp.arange(seq_parts, dtype=jnp.int32),
        2 * seq_parts,
    )
    back_cos, back_sin = angles(
        jnp.arange(seq_parts, dtype=jnp.int32),
        jnp.arange(2 * seq_parts, dtype=jnp.int32),
        2 * seq_parts,
    )
    inner_cos, inner_sin = angles(
        jnp.arange(tok_rows, dtype=jnp.int32), jnp.arange(tok_rows, dtype=jnp.int32), tok_rows
    )
    fwd_cos, fwd_sin = angles(
        jnp.arange(2 * seq_parts, dtype=jnp.int32),
        my_index * sub_rows + jnp.arange(sub_rows, dtype=jnp.int32),
        padded,
    )
    inv_cos, inv_sin = angles(
        2 * my_index + jnp.arange(2, dtype=jnp.int32), jnp.arange(tok_rows, dtype=jnp.int32), padded
    )
    position, window, kernel, gated_grad = home_inputs(
        gate, grad_y, filt, decay, my_index, tok_rows, length, norm_scale
    )
    fields = jnp.stack([values.astype(jnp.float32), kernel, gated_grad])[:, None]
    half_spectrum = forward_outer(
        lax.all_to_all(fields, "seq", split_axis=2, concat_axis=1, tiled=True),
        outer_cos,
        outer_sin,
        fwd_cos,
        fwd_sin,
    )
    spectrum = forward_inner(
        lax.all_to_all(
            half_spectrum[:, :, :, None], "seq", split_axis=2, concat_axis=3, tiled=True
        ),
        inner_cos,
        inner_sin,
    )
    inverted = inverse_inner(products(spectrum), inner_cos, inner_sin, inv_cos, inv_sin)
    fields_away = inverse_outer(
        lax.all_to_all(inverted[:, :, None], "seq", split_axis=4, concat_axis=2, tiled=True),
        back_cos,
        back_sin,
        padded,
    )
    returned = lax.all_to_all(fields_away, "seq", split_axis=1, concat_axis=2, tiled=True)
    d_values, d_gate, gated_out, d_filt, decay_part = home_results(
        returned[0, 0],
        returned[1, 0],
        returned[2, 0],
        gate,
        grad_y,
        position,
        window,
        kernel,
        norm_scale,
    )
    decay_grad = -norm_scale * lax.psum(decay_part, "seq")
    term = lax.dot_general(
        full_grad, gated_out, (((0,), (0,)), ((), ())), preferred_element_type=jnp.float32
    )
    d_out_weight = lax.psum_scatter(term * norm_scale, "seq", scatter_dimension=0, tiled=True)
    return (d_values, d_gate, d_filt, decay_grad, d_out_weight)


def solution(mesh):
    in_specs = (
        P("seq", "tp"),
        P("seq", "tp"),
        P("seq", "tp"),
        P(None, "tp"),
        P("seq", "tp"),
        P("tp"),
    )
    out_specs = (P("seq", "tp"), P("seq", "tp"), P("seq", "tp"), P("tp"), P("seq", "tp"))
    return jax.shard_map(
        on_device, mesh=mesh, in_specs=in_specs, out_specs=out_specs, check_vma=False
    )
```

profile of v0, /device:TPU:4, one launch (start us, length us, event | category | flops | bytes accessed | tf_op | source)
XLA Modules:
  0.0 709.1 jit_solution(6259057081510441585)
XLA Ops:
  10.8 59.6 %all-gather.2.cloned.1.call-done = bf16[256,4096]{1,0:T(8,128)(2,1)} async-done(((bf16[256,512]{1,0:T(8,128)(2,1)}), bf16[256,4096]{1,0:T(8,128)(2,1)}) %all-gather.2.cloned.1.call-update) | async-done | bytes 2097168 | tf_op jit(solution)/shard_map/all_gather | solution.py:111
  70.5 4.1 fusion.30
  78.3 9.1 %all-to-all-start = ((f32[3,1,256,512]{3,1,0,2:T(1,128)}), f32[3,1,256,512]{3,1,0,2:T(1,128)S(1)}, u32[]{:S(2)}, u32[]{:S(2)}) async-start(f32[3,1,256,512]{3,1,0,2:T(1,128)} %copy.66), calls=%async_computation | async-start | bytes 3145728 | tf_op jit(solution)/shard_map/all_to_all | solution.py:139
  87.6 38.9 %all-to-all-done = f32[3,1,256,512]{3,1,0,2:T(1,128)S(1)} async-done(((f32[3,1,256,512]{3,1,0,2:T(1,128)}), f32[3,1,256,512]{3,1,0,2:T(1,128)S(1)}, u32[]{:S(2)}, u32[]{:S(2)}) %all-to-all-start) | async-done | bytes 1572896 | tf_op jit(solution)/shard_map/all_to_all | solution.py:139
  126.6 4.0 fusion.26
  130.6 4.9 fusion.9
  136.8 6.7 copy.70
  143.5 4.9 all-to-all-start.1
  148.6 140.6 %all-to-all-done.1 = f32[2,3,64,1,8,512]{5,4,1,0,3,2:T(8,128)} async-done(((f32[2,3,64,1,8,512]{5,4,1,0,3,2:T(8,128)}), f32[2,3,64,1,8,512]{5,4,1,0,3,2:T(8,128)}, u32[]{:S(2)}, u32[]{:S(2)}) %all-to-all-start.1) | async-done | bytes 6291488 | tf_op jit(solution)/shard_map/all_to_all | solution.py:146
  294.1 6.3 fusion.2
  300.4 6.5 fusion
  306.9 6.4 add_bitcast_fusion.1
  313.3 6.7 subtract_bitcast_fusion.1
  328.3 4.3 fusion.24
  332.6 4.3 subtract_bitcast_fusion
  340.0 10.4 %copy.78 = f32[2,3,1,2,256,512]{5,3,1,0,2,4:T(2,128)} copy(f32[2,3,1,2,256,512]{4,5,3,1,0,2:T(8,128)} %maximum_bitcast_fusion.1) | data formatting | bytes 12582912 | tf_op jit(solution)/shard_map/broadcast_in_dim | solution.py:154
  350.4 148.1 %all_to_all.51 = f32[2,3,1,2,256,512]{5,3,1,0,2,4:T(2,128)S(1)} all-to-all(f32[2,3,1,2,256,512]{5,3,1,0,2,4:T(2,128)} %copy.78), channel_id=1, replica_groups=mesh['seq'=32,'tp'=8] {'seq'}, dimensions={4} | all-to-all | bytes 12582912 | tf_op jit(solution)/shard_map/all_to_all | solution.py:154
  508.7 5.2 fusion.67
  513.9 4.1 copy.81
  518.0 4.1 squeeze.28
  526.5 44.9 %all_to_all.52 = f32[3,32,8,512]{3,2,0,1:T(8,128)S(1)} all-to-all(f32[3,32,8,512]{3,2,0,1:T(8,128)S(1)} %copy.82), channel_id=1, replica_groups=mesh['seq'=32,'tp'=8] {'seq'}, dimensions={1} | all-to-all | bytes 3145728 | tf_op jit(solution)/shard_map/all_to_all | solution.py:159
  571.3 4.5 multiply_bitcast_fusion
  578.2 53.1 %psum.7 = f32[512]{0:T(512)S(1)} all-reduce(f32[512]{0:T(512)S(1)} %get-tuple-element.44), channel_id=1, replica_groups=mesh['seq'=32,'tp'=8] {'seq'}, use_global_device_ids=true, to_apply=%region_1.2 | all-reduce | flops 512 | bytes 4096 | tf_op jit(solution)/shard_map/psum | solution.py:171
  632.6 67.7 %reduce-scatter.2.cloned.1.call-done = f32[128,512]{0,1:T(8,128)} async-done(((f32[4096,512]{0,1:T(8,128)}), f32[128,512]{0,1:T(8,128)}) %reduce-scatter.2.cloned.1.call-update) | async-done | bytes 262160 | tf_op jit(solution)/shard_map/reduce_scatter | solution.py:175
  (46 shorter events, 45.2 us)
Async XLA Ops:
  7.2 63.3 %all-gather.2.cloned.1.call-start = ((), (), s32[]{:S(2)}) async-start(), calls=%async_computation.5 | async-start | bytes 2359296 | tf_op jit(solution)/shard_map/all_gather | solution.py:111
  10.8 64.5 %copy-start.5 = (bf16[256,512]{1,0:T(8,128)(2,1)S(1)}, bf16[256,512]{1,0:T(8,128)(2,1)}, u32[]{:S(2)}) copy-start(bf16[256,512]{1,0:T(8,128)(2,1)} %param.7) | copy-start | bytes 786436
  74.5 0.8 copy-start.2
  78.3 48.2 %all-to-all-start = ((f32[3,1,256,512]{3,1,0,2:T(1,128)}), f32[3,1,256,512]{3,1,0,2:T(1,128)S(1)}, u32[]{:S(2)}, u32[]{:S(2)}) async-start(f32[3,1,256,512]{3,1,0,2:T(1,128)} %copy.66), calls=%async_computation | async-start | bytes 3145728 | tf_op jit(solution)/shard_map/all_to_all | solution.py:139
  143.5 145.7 %all-to-all-start.1 = ((f32[2,3,64,1,8,512]{5,4,1,0,3,2:T(8,128)}), f32[2,3,64,1,8,512]{5,4,1,0,3,2:T(8,128)}, u32[]{:S(2)}, u32[]{:S(2)}) async-start(f32[2,3,64,1,8,512]{5,4,1,0,3,2:T(8,128)} %copy.70), calls=%async_computation.1 | async-start | bytes 12582912 | tf_op jit(solution)/shard_map/all_to_all | solution.py:146
  148.4 551.8 %reduce-scatter.2.cloned.1.call-start = ((), (), s32[]{:S(2)}) async-start(), calls=%async_computation.6 | async-start | bytes 8650752 | tf_op jit(solution)/shard_map/reduce_scatter | solution.py:175
  508.7 5.2 copy-start
  525.5 45.8 %copy-start.4 = (bf16[256,4096]{1,0:T(8,128)(2,1)S(1)}, bf16[256,4096]{1,0:T(8,128)(2,1)}, u32[]{:S(2)}) copy-start(bf16[256,4096]{1,0:T(8,128)(2,1)} %all-gather.2.cloned.1.call-done) | copy-start | bytes 6291460
  575.9 1.0 copy-start.1
  575.9 1.2 copy-start.3
Sparse Core Ops, SparseCore 0:
  10.5 59.9 all-gather.1
  576.0 124.1 reduce-scatter.1
where the time goes:
time: 713 us; the launch traced here: 709 us
  waiting for transfers between devices  308 us (43%)
  blocking collectives  246 us (35%)
  matrix products  68.1 us (10%)
  local copies, waits for them, and re-layouts  48.6 us (7%)
  between operations  14.5 us (2%)
  starting transfers between devices  14.1 us (2%)
  other arithmetic  10.2 us (1%)
    all_to_all x1, blocking collectives, on_device(): lax.all_to_all(inverted[:, :, None], 'seq', split_axis=4, concat_axis=2,...  148 us
    all_to_all x1, waiting for transfers between devices, on_device(): lax.all_to_all(half_spectrum[:, :, :, None], 'seq', split_axis=2, concat_...  141 us
    reduce_scatter x1, waiting for transfers between devices, on_device(): lax.psum_scatter(term * norm_scale, 'seq', scatter_dimension=0, tiled=True)  67.7 us
    all_gather x1, waiting for transfers between devices, on_device(): full_grad = lax.all_gather(out_grad, 'tp', axis=1, tiled=True)  59.6 us
    psum x1, blocking collectives, on_device(): decay_grad = -norm_scale * lax.psum(decay_part, 'seq')  53.1 us
    all_to_all x1, blocking collectives, on_device(): lax.all_to_all(fields_away, 'seq', split_axis=1, concat_axis=2, tiled=True)  44.9 us
    all_to_all x1, waiting for transfers between devices, on_device(): lax.all_to_all(fields, 'seq', split_axis=2, concat_axis=1, tiled=True)  38.9 us
  transfers between devices with their start and end apart: 4, of which 4 were waited for; matrix products, arithmetic and copies ran while one was open for 1% of the time, Pallas kernels for 0%

commit v1 on v0

--- a/solution.py
+++ b/solution.py
@@ -108,7 +108,9 @@
     length = tok_rows * seq_parts
     padded = 2 * length
     norm_scale = 1.0 / math.sqrt(length)
-    full_grad = lax.all_gather(out_grad, "tp", axis=1, tiled=True)
+    full_grad = jnp.concatenate(
+        lax.all_to_all(jnp.stack([out_grad] * lax.axis_size("tp")), "tp", 0, 0), axis=1
+    )
     grad_y = jnp.dot(full_grad, out_weight, preferred_element_type=jnp.float32).astype(jnp.bfloat16)
     outer_cos, outer_sin = angles(
         jnp.arange(2 * seq_parts, dtype=jnp.int32),

time: 713 us -> 686 us (0.962)
  waiting for transfers between devices: 308 us -> 272 us
  starting transfers between devices: 14.1 us -> 22 us
    all_gather x1 -> x0, waiting for transfers between devices: 59.6 us -> none  [on_device(): full_grad = lax.all_gather(out_grad, 'tp', axis=1, tiled=True)]
    all_to_all x0 -> x1, waiting for transfers between devices: none -> 25.7 us  [on_device(): lax.all_to_all(jnp.stack([out_grad] * lax.axis_size('tp')), 'tp', 0, 0)]
    all_to_all x0 -> x1, starting transfers between devices: none -> 7.43 us  [on_device(): lax.all_to_all(jnp.stack([out_grad] * lax.axis_size('tp')), 'tp', 0, 0)]
  transfers between devices with their start and end apart: 4 -> 4, of which waited for: 4 -> 4; matrix products, arithmetic and copies ran while one was open for 1% -> 0% of each run, Pallas kernels for 0% -> 0%
where the time goes in v1:
time: 686 us; the launch traced here: 682 us
  waiting for transfers between devices  272 us (40%)
  blocking collectives  246 us (36%)
  matrix products  68.2 us (10%)
  local copies, waits for them, and re-layouts  50.8 us (7%)
  starting transfers between devices  22 us (3%)
  between operations  14.6 us (2%)
  other arithmetic  7.54 us (1%)
    all_to_all x1, blocking collectives, on_device(): lax.all_to_all(inverted[:, :, None], 'seq', split_axis=4, concat_axis=2,...  148 us
    all_to_all x1, waiting for transfers between devices, on_device(): lax.all_to_all(half_spectrum[:, :, :, None], 'seq', split_axis=2, concat_...  141 us
    reduce_scatter x1, waiting for transfers between devices, on_device(): lax.psum_scatter(term * norm_scale, 'seq', scatter_dimension=0, tiled=True)  67.3 us
    psum x1, blocking collectives, on_device(): decay_grad = -norm_scale * lax.psum(decay_part, 'seq')  53 us
    all_to_all x1, blocking collectives, on_device(): lax.all_to_all(fields_away, 'seq', split_axis=1, concat_axis=2, tiled=True)  44.9 us
    all_to_all x1, waiting for transfers between devices, on_device(): lax.all_to_all(fields, 'seq', split_axis=2, concat_axis=1, tiled=True)  38.9 us
    all_to_all x1, waiting for transfers between devices, on_device(): lax.all_to_all(jnp.stack([out_grad] * lax.axis_size('tp')), 'tp', 0, 0)  25.7 us
  transfers between devices with their start and end apart: 4, of which 4 were waited for; matrix products, arithmetic and copies ran while one was open for 0% of the time, Pallas kernels for 0%

profile of v1, /device:TPU:4, one launch (start us, length us, event | category | flops | bytes accessed | tf_op | source)
XLA Modules:
  0.0 681.7 jit_solution(5480945717035879626)
XLA Ops:
  9.8 7.4 %all-to-all-start = ((bf16[8,256,512]{1,2,0:T(8,128)(2,1)}), bf16[8,256,512]{1,2,0:T(8,128)(2,1)S(1)}, u32[]{:S(2)}, u32[]{:S(2)}) async-start(bf16[8,256,512]{1,2,0:T(8,128)(2,1)} %stack.65), calls=%async_computation | async-start | bytes 4194304 | tf_op jit(solution)/shard_map/all_to_all | solution.py:112
  17.3 25.7 %all-to-all-done = bf16[8,256,512]{1,2,0:T(8,128)(2,1)S(1)} async-done(((bf16[8,256,512]{1,2,0:T(8,128)(2,1)}), bf16[8,256,512]{1,2,0:T(8,128)(2,1)S(1)}, u32[]{:S(2)}, u32[]{:S(2)}) %all-to-all-start) | async-done | bytes 2097184 | tf_op jit(solution)/shard_map/all_to_all | solution.py:112
  43.0 4.2 fusion.30
  50.9 9.7 %all-to-all-start.1 = ((f32[3,1,256,512]{3,1,0,2:T(1,128)}), f32[3,1,256,512]{3,1,0,2:T(1,128)S(1)}, u32[]{:S(2)}, u32[]{:S(2)}) async-start(f32[3,1,256,512]{3,1,0,2:T(1,128)} %copy.70), calls=%async_computation.1 | async-start | bytes 3145728 | tf_op jit(solution)/shard_map/all_to_all | solution.py:141
  60.7 38.9 %all-to-all-done.1 = f32[3,1,256,512]{3,1,0,2:T(1,128)S(1)} async-done(((f32[3,1,256,512]{3,1,0,2:T(1,128)}), f32[3,1,256,512]{3,1,0,2:T(1,128)S(1)}, u32[]{:S(2)}, u32[]{:S(2)}) %all-to-all-start.1) | async-done | bytes 1572896 | tf_op jit(solution)/shard_map/all_to_all | solution.py:141
  103.8 5.0 fusion.9
  110.0 6.7 copy.74
  116.7 4.9 all-to-all-start.2
  121.8 140.6 %all-to-all-done.2 = f32[2,3,64,1,8,512]{5,4,1,0,3,2:T(8,128)} async-done(((f32[2,3,64,1,8,512]{5,4,1,0,3,2:T(8,128)}), f32[2,3,64,1,8,512]{5,4,1,0,3,2:T(8,128)}, u32[]{:S(2)}, u32[]{:S(2)}) %all-to-all-start.2) | async-done | bytes 6291488 | tf_op jit(solution)/shard_map/all_to_all | solution.py:148
  267.2 6.3 fusion.2
  273.5 6.5 fusion
  280.0 6.4 add_bitcast_fusion.1
  286.4 6.7 subtract_bitcast_fusion.1
  301.4 4.3 fusion.24
  305.8 4.3 subtract_bitcast_fusion
  313.1 10.3 %copy.82 = f32[2,3,1,2,256,512]{5,3,1,0,2,4:T(2,128)} copy(f32[2,3,1,2,256,512]{4,5,3,1,0,2:T(8,128)} %maximum_bitcast_fusion.1) | data formatting | bytes 12582912 | tf_op jit(solution)/shard_map/broadcast_in_dim | solution.py:156
  323.4 148.1 %all_to_all.56 = f32[2,3,1,2,256,512]{5,3,1,0,2,4:T(2,128)S(1)} all-to-all(f32[2,3,1,2,256,512]{5,3,1,0,2,4:T(2,128)} %copy.82), channel_id=1, replica_groups=mesh['seq'=32,'tp'=8] {'seq'}, dimensions={4} | all-to-all | bytes 12582912 | tf_op jit(solution)/shard_map/all_to_all | solution.py:156
  481.7 5.2 fusion.67
  486.9 4.1 copy.85
  491.0 4.1 squeeze.28
  499.5 44.9 %all_to_all.57 = f32[3,32,8,512]{3,2,0,1:T(8,128)S(1)} all-to-all(f32[3,32,8,512]{3,2,0,1:T(8,128)S(1)} %copy.86), channel_id=1, replica_groups=mesh['seq'=32,'tp'=8] {'seq'}, dimensions={1} | all-to-all | bytes 3145728 | tf_op jit(solution)/shard_map/all_to_all | solution.py:161
  544.4 4.6 multiply_bitcast_fusion
  551.3 53.0 %psum.7 = f32[512]{0:T(512)S(1)} all-reduce(f32[512]{0:T(512)S(1)} %get-tuple-element.44), channel_id=1, replica_groups=mesh['seq'=32,'tp'=8] {'seq'}, use_global_device_ids=true, to_apply=%region_1.2 | all-reduce | flops 512 | bytes 4096 | tf_op jit(solution)/shard_map/psum | solution.py:173
  605.6 67.3 %reduce-scatter.2.cloned.1.call-done = f32[128,512]{0,1:T(8,128)} async-done(((f32[4096,512]{0,1:T(8,128)}), f32[128,512]{0,1:T(8,128)}) %reduce-scatter.2.cloned.1.call-update) | async-done | bytes 262160 | tf_op jit(solution)/shard_map/reduce_scatter | solution.py:177
  (54 shorter events, 48.1 us)
Async XLA Ops:
  8.3 8.9 %copy-start.9 = (f32[512]{0:T(512)S(1)}, f32[512]{0:T(512)}, u32[]{:S(2)}) copy-start(f32[512]{0:T(512)} %param.11) | copy-start | bytes 6148
  8.3 8.9 %copy-start.8 = (bf16[256,512]{1,0:T(8,128)(2,1)S(1)}, bf16[256,512]{1,0:T(8,128)(2,1)}, u32[]{:S(2)}) copy-start(bf16[256,512]{1,0:T(8,128)(2,1)} %param.6) | copy-start | bytes 786436
  9.8 33.2 %all-to-all-start = ((bf16[8,256,512]{1,2,0:T(8,128)(2,1)}), bf16[8,256,512]{1,2,0:T(8,128)(2,1)S(1)}, u32[]{:S(2)}, u32[]{:S(2)}) async-start(bf16[8,256,512]{1,2,0:T(8,128)(2,1)} %stack.65), calls=%async_computation | async-start | bytes 4194304 | tf_op jit(solution)/shard_map/all_to_all | solution.py:112
  43.0 4.2 copy-start.1
  43.0 4.2 copy-start.3
  43.0 4.3 copy-start.7
  47.2 0.8 copy-start.5
  50.9 48.7 %all-to-all-start.1 = ((f32[3,1,256,512]{3,1,0,2:T(1,128)}), f32[3,1,256,512]{3,1,0,2:T(1,128)S(1)}, u32[]{:S(2)}, u32[]{:S(2)}) async-start(f32[3,1,256,512]{3,1,0,2:T(1,128)} %copy.70), calls=%async_computation.1 | async-start | bytes 3145728 | tf_op jit(solution)/shard_map/all_to_all | solution.py:141
  116.7 145.7 %all-to-all-start.2 = ((f32[2,3,64,1,8,512]{5,4,1,0,3,2:T(8,128)}), f32[2,3,64,1,8,512]{5,4,1,0,3,2:T(8,128)}, u32[]{:S(2)}, u32[]{:S(2)}) async-start(f32[2,3,64,1,8,512]{5,4,1,0,3,2:T(8,128)} %copy.74), calls=%async_computation.2 | async-start | bytes 12582912 | tf_op jit(solution)/shard_map/all_to_all | solution.py:148
  121.6 551.3 %reduce-scatter.2.cloned.1.call-start = ((), (), s32[]{:S(2)}) async-start(), calls=%async_computation.6 | async-start | bytes 8650752 | tf_op jit(solution)/shard_map/reduce_scatter | solution.py:177
  481.7 5.2 copy-start
  498.6 45.8 %copy-start.2 = (bf16[8,256,512]{1,2,0:T(8,128)(2,1)S(1)}, bf16[8,256,512]{1,2,0:T(8,128)(2,1)}, u32[]{:S(2)}) copy-start(bf16[8,256,512]{1,2,0:T(8,128)(2,1)} %copy-done.1) | copy-start | bytes 6291460
  548.9 1.0 copy-start.4
  548.9 1.2 copy-start.6
Sparse Core Ops, SparseCore 0:
  549.1 123.7 reduce-scatter.1
